TPU v7x, 512 devices: a whole 4x4x16 slice. The times are simulated.
512 devices in a mesh: seq: 4 (over z_lo), fsdp: 32 (over z_hi, y, core), dp: 4 (over x).
Axes of the slice: x: 4, y: 4, z: 16 (z_hi: 4, z_lo: 4; z = z_hi * 4 + z_lo), core: 2. Of those that a mesh axis runs over, the one named last changes fastest.
Arguments:
- query: bfloat16 [128, 768, 1024], P(('fsdp', 'dp'), 'seq'), may hold values from -6 to 6
- key: bfloat16 [128, 768, 1024], P(('fsdp', 'dp'), 'seq'), may hold values from -6 to 6
- value: bfloat16 [128, 768, 1024], P(('fsdp', 'dp'), 'seq'), may hold values from -4 to 4
- out_weight: bfloat16 [1024, 2048], P('fsdp'), may hold values from -0.1875 to 0.1875
- out_grad: bfloat16 [128, 768, 2048], P(('fsdp', 'dp'), 'seq'), may hold values from -5 to 5
- block_ids: int32 [8], P('seq'), may hold values from 0 to 7, as said below
Outputs:
- query_grad: bfloat16 [128, 768, 1024], P(('fsdp', 'dp'), 'seq')
- key_grad: bfloat16 [128, 768, 1024], P(('fsdp', 'dp'), 'seq')
- value_grad: bfloat16 [128, 768, 1024], P(('fsdp', 'dp'), 'seq')
- weight_grad: bfloat16 [1024, 2048], P('fsdp')
Inputs may be any that keep to these rules, and one draw needn't show every extreme that they name: `block_ids`: each number 0 to 7 appears once, and entries 2 i and 2 i + 1 always sum to 7.
All inputs are finite; a program needn't handle non-finite values.
Results may differ from a plain program's by a relative error of at most 0.027.
Values may be sent and summed in bfloat16 or wider, within the bound.
No kernel may reach another device: no remote copies, remote signals or barrier semaphores. Data moves between devices by JAX's collectives and lax.ppermute only.
A program may use at most 64 MiB of HBM per device.

v0:
```python
import math
import jax
import jax.numpy as jnp
from jax import lax
from jax.sharding import PartitionSpec as P

HEADS = 8
HD = 128


def positions_of(block_list, block_rows):
    offsets = jnp.arange(block_rows, dtype=jnp.int32)
    return (block_list[:, None] * block_rows + offsets[None, :]).reshape(-1)


def shards(query, key, value, out_weight, out_grad, block_ids):
    tokens_here = query.shape[1]
    width_heads = query.shape[2]
    block_rows = tokens_here // block_ids.shape[0]
    score_scale = 1.0 / math.sqrt(HD)
    all_blocks = lax.all_gather(block_ids, "seq", axis=0, tiled=True)
    query_pos = positions_of(block_ids, block_rows)
    every_pos = positions_of(all_blocks, block_rows)
    key_all, value_all = (
        lax.all_gather(key, "seq", axis=1, tiled=True),
        lax.all_gather(value, "seq", axis=1, tiled=True),
    )
    query_heads = query[0].reshape(tokens_here, HEADS, HD)
    key_heads = key_all[0].reshape(-1, HEADS, HD)
    value_heads = value_all[0].reshape(-1, HEADS, HD)
    scores = (
        jnp.einsum("thd,khd->htk", query_heads, key_heads, preferred_element_type=jnp.float32)
        * score_scale
    )
    allowed = every_pos[None, :] <= query_pos[:, None]
    scores = jnp.where(allowed[None], scores, -jnp.inf)
    row_top = jnp.max(scores, axis=2, keepdims=True)
    row_total = jnp.sum(jnp.exp(scores - row_top), axis=2, keepdims=True)
    log_total = row_top + jnp.log(row_total)
    weights = jnp.exp(scores - log_total)
    weights_low = weights.astype(jnp.bfloat16)
    attended = jnp.einsum(
        "htk,khd->thd", weights_low, value_heads, preferred_element_type=jnp.float32
    ).astype(jnp.bfloat16)
    grad_rows = out_grad[0]
    attn_grad = lax.dot_general(
        grad_rows,
        lax.all_gather(out_weight, "fsdp", axis=0, tiled=True),
        (((1,), (1,)), ((), ())),
        preferred_element_type=jnp.float32,
    ).astype(jnp.bfloat16)
    attended_flat = attended.reshape(tokens_here, width_heads)
    weight_shard = lax.psum_scatter(
        lax.dot_general(
            attended_flat, grad_rows, (((0,), (0,)), ((), ())), preferred_element_type=jnp.float32
        ).astype(jnp.bfloat16),
        "fsdp",
        scatter_dimension=0,
        tiled=True,
    ).astype(jnp.float32)
    token_count = tokens_here * lax.axis_size("seq") * lax.axis_size("fsdp") * lax.axis_size("dp")
    weight_grad = (lax.psum(weight_shard, ("seq", "dp")) * (1.0 / math.sqrt(token_count))).astype(
        jnp.bfloat16
    )
    grad_heads = attn_grad.reshape(tokens_here, HEADS, HD)
    row_delta = jnp.einsum("thd,thd->ht", grad_heads, attended, preferred_element_type=jnp.float32)
    prob_grad = jnp.einsum(
        "thd,khd->htk", grad_heads, value_heads, preferred_element_type=jnp.float32
    )
    score_grad = (weights * (prob_grad - row_delta[:, :, None])).astype(jnp.bfloat16)
    query_grad = (
        jnp.einsum("htk,khd->thd", score_grad, key_heads, preferred_element_type=jnp.float32)
        * score_scale
    ).astype(jnp.bfloat16)
    query_all, grad_all = (
        lax.all_gather(query, "seq", axis=1, tiled=True),
        lax.all_gather(attn_grad[None], "seq", axis=1, tiled=True),
    )
    totals_all, deltas_all = (
        lax.all_gather(log_total[:, :, 0][None], "seq", axis=2, tiled=True),
        lax.all_gather(row_delta[None], "seq", axis=2, tiled=True),
    )
    local_keys = key[0].reshape(tokens_here, HEADS, HD)
    local_values = value[0].reshape(tokens_here, HEADS, HD)
    gathered_queries = query_all[0].reshape(-1, HEADS, HD)
    gathered_grads = grad_all[0].reshape(-1, HEADS, HD)
    back_scores = (
        jnp.einsum("khd,qhd->hkq", local_keys, gathered_queries, preferred_element_type=jnp.float32)
        * score_scale
    )
    back_allowed = query_pos[:, None] <= every_pos[None, :]
    back_scores = jnp.where(back_allowed[None], back_scores, -jnp.inf)
    back_weights = jnp.exp(back_scores - totals_all[0][:, None, :])
    back_low = back_weights.astype(jnp.bfloat16)
    back_prob_grad = jnp.einsum(
        "qhd,khd->hkq", gathered_grads, local_values, preferred_element_type=jnp.float32
    )
    back_score_grad = (back_weights * (back_prob_grad - deltas_all[0][:, None, :])).astype(
        jnp.bfloat16
    )
    key_grad = (
        jnp.einsum(
            "hkq,qhd->khd", back_score_grad, gathered_queries, preferred_element_type=jnp.float32
        )
        * score_scale
    ).astype(jnp.bfloat16)
    value_grad = jnp.einsum(
        "hkq,qhd->khd", back_low, gathered_grads, preferred_element_type=jnp.float32
    ).astype(jnp.bfloat16)
    return (
        query_grad.reshape(tokens_here, width_heads)[None],
        key_grad.reshape(tokens_here, width_heads)[None],
        value_grad.reshape(tokens_here, width_heads)[None],
        weight_grad,
    )


def solution(mesh):
    in_specs = (
        P(("fsdp", "dp"), "seq", None),
        P(("fsdp", "dp"), "seq", None),
        P(("fsdp", "dp"), "seq", None),
        P("fsdp", None),
        P(("fsdp", "dp"), "seq", None),
        P("seq"),
    )
    out_specs = (
        P(("fsdp", "dp"), "seq", None),
        P(("fsdp", "dp"), "seq", None),
        P(("fsdp", "dp"), "seq", None),
        P("fsdp", None),
    )
    return jax.shard_map(shards, mesh=mesh, in_specs=in_specs, out_specs=out_specs, check_vma=False)
```

profile of v0, /device:TPU:16, one launch (start us, length us, event | category | flops | bytes accessed | tf_op | source)
XLA Modules:
  0.0 531.4 jit_solution(5790894048885190867)
XLA Ops:
  7.2 0.7 all-gather.13.cloned.1.call-update
  8.0 0.7 all-gather.11.cloned.1.call-update
  8.7 0.7 all-gather.15.cloned.1.call-update
  9.4 0.5 all-gather.17.cloned.1.call-update
  10.0 1.3 dynamic-slice
  12.0 0.9 dynamic-update-slice
  12.8 9.1 %all-reduce = s32[8]{0:T(128)S(1)} all-reduce(s32[8]{0:T(128)S(1)} %dynamic-update-slice), channel_id=1, replica_groups=mesh['seq'=4,'fsdp'=32,'dp'=4] {'seq'}, use_global_device_ids=true, to_apply=%add | all-reduce | flops 8 | bytes 64
  21.9 0.1 iota_add_fusion
  22.0 0.1 add.65
  22.1 0.7 broadcast_multiply_fusion
  22.8 0.1 iota_add_fusion.1
  22.8 0.1 add.69
  22.9 1.1 copy.64
  24.0 86.7 %all-gather.13.cloned.1.call-done = bf16[1024,2048]{1,0:T(8,128)(2,1)} async-done(((bf16[32,2048]{1,0:T(8,128)(2,1)}), bf16[1024,2048]{1,0:T(8,128)(2,1)}) %all-gather.13.cloned.1.call-update) | async-done | bytes 4194320 | tf_op jit(solution)/shard_map/all_gather | solution.py:48
  110.6 4.5 convolution_convert_fusion.1
  115.2 0.2 broadcast_compare_fusion
  115.4 39.8 %all-gather.11.cloned.1.call-done = bf16[1,768,1024]{2,1,0:T(8,128)(2,1)} async-done(((bf16[1,192,1024]{2,1,0:T(8,128)(2,1)}), bf16[1,768,1024]{2,1,0:T(8,128)(2,1)}) %all-gather.11.cloned.1.call-update) | async-done | bytes 1572880 | tf_op jit(solution)/shard_map/all_gather | solution.py:25
  155.2 1.7 copy.28
  157.0 46.7 %all-gather.15.cloned.1.call-done = bf16[1,768,1024]{2,1,0:T(8,128)(2,1)} async-done(((bf16[1,192,1024]{2,1,0:T(8,128)(2,1)}), bf16[1,768,1024]{2,1,0:T(8,128)(2,1)}) %all-gather.15.cloned.1.call-update) | async-done | bytes 1572880 | tf_op jit(solution)/shard_map/all_gather | solution.py:26
  203.7 2.6 copy.31
  206.3 1.0 fusion.3
  207.3 1.2 exponential_reduce_fusion
  208.6 0.1 copy.65
  208.6 0.1 bitcast_convert_fusion
  208.7 1.1 copy-done.3
  209.9 1.6 multiply_reduce_fusion
  211.6 3.4 convolution_convert_fusion
  215.0 0.8 copy.67
  215.9 13.1 %all-gather.3 = f32[4,192,8]{1,2,0:T(8,128)S(1)} all-gather(f32[1,192,8]{1,2,0:T(8,128)S(1)} %bitcast.115), channel_id=2, replica_groups=mesh['seq'=4,'fsdp'=32,'dp'=4] {'seq'}, dimensions={0}, use_global_device_ids=true | all-gather | bytes 30720 | tf_op jit(solution)/shard_map/all_gather | solution.py:80
  229.0 0.1 reshape.140
  229.1 22.9 %all-gather.17.cloned.1.call-done = bf16[1,768,1024]{2,1,0:T(8,128)(2,1)} async-done(((bf16[1,192,1024]{2,1,0:T(8,128)(2,1)}), bf16[1,768,1024]{2,1,0:T(8,128)(2,1)}) %all-gather.17.cloned.1.call-update) | async-done | bytes 1572880 | tf_op jit(solution)/shard_map/all_gather | solution.py:76
  252.0 1.7 copy.37
  253.7 2.9 fusion.72
  256.7 6.3 %fusion.56 = bf16[192,8,128]{2,0,1:T(8,128)(2,1)} fusion(bf16[768,8,128]{0,2,1:T(8,128)(2,1)} %bitcast.105, f32[8,192,768]{2,1,0:T(8,128)} %copy-done.1, f32[8,192]{1,0:T(8,128)S(1)} %get-tuple-element.8, f32[8,192]{1,0:T(8,128)S(1)} %log_add_fusion, pred[192,768]{1,0:T(8,128)(4,1)S(1)} %get-tuple-element.5, bf16[768,8,128]{0,2,1:T(8,128)(2,1)} %bitcast.106, ...), kind=kOutput, calls=%fused_computation.39 | convolution fusion | flops 611450880 | bytes 8810496 | tf_op jit(solution)/shard_map/htk,khd->thd/dot_general | solution.py:72
  262.9 1.3 copy.36
  264.2 0.9 broadcast_in_dim_reshape.6
  265.1 13.4 %all-gather.4 = f32[4,192,8]{1,2,0:T(8,128)S(1)} all-gather(f32[1,192,8]{1,2,0:T(8,128)S(1)} %bitcast.119), channel_id=4, replica_groups=mesh['seq'=4,'fsdp'=32,'dp'=4] {'seq'}, dimensions={0}, use_global_device_ids=true | all-gather | bytes 30720 | tf_op jit(solution)/shard_map/all_gather | solution.py:81
  278.5 0.1 reshape.142
  278.6 22.4 %all-gather.19.cloned.1.call-done = bf16[768,1024]{1,0:T(8,128)(2,1)} async-done(((bf16[192,1024]{1,0:T(8,128)(2,1)}), bf16[768,1024]{1,0:T(8,128)(2,1)}) %all-gather.19.cloned.1.call-update) | async-done | bytes 1572880 | tf_op jit(solution)/shard_map/all_gather | solution.py:77
  301.0 4.8 fusion.51
  305.8 0.3 copy.45
  306.1 0.9 broadcast_in_dim_reshape.14
  307.0 4.2 fusion.57
  311.3 0.3 copy.47
  311.5 0.9 broadcast_in_dim_reshape.15
  312.4 129.9 %reduce-scatter.2.cloned.1.call-done = bf16[32,2048]{1,0:T(8,128)(2,1)} async-done(((bf16[1024,2048]{1,0:T(8,128)(2,1)}), bf16[32,2048]{1,0:T(8,128)(2,1)}) %reduce-scatter.2.cloned.1.call-update) | async-done | bytes 131088 | tf_op jit(solution)/shard_map/reduce_scatter | solution.py:53
  442.3 81.5 %all-reduce.2 = f32[32,2048]{1,0:T(8,128)S(1)} all-reduce(bf16[32,2048]{1,0:T(8,128)(2,1)} %reduce-scatter.2.cloned.1.call-done), channel_id=1, replica_groups=mesh['seq'=4,'fsdp'=32,'dp'=4] {'seq','dp'}, use_global_device_ids=true, to_apply=%region_3.4 | all-reduce | flops 65536 | bytes 393216 | tf_op jit(solution)/shard_map/psum | solution.py:62
  523.9 0.7 multiply_convert_fusion.8
  (29 shorter events, 0.4 us)
Async XLA Ops:
  7.2 103.5 %copy-start = (bf16[1,192,2048]{2,1,0:T(8,128)(2,1)S(1)}, bf16[1,192,2048]{2,1,0:T(8,128)(2,1)}, u32[]{:S(2)}) copy-start(bf16[1,192,2048]{2,1,0:T(8,128)(2,1)} %param.10) | copy-start | bytes 2359300
  7.2 103.5 %all-gather.13.cloned.1.call-start = ((), (), s32[]{:S(2)}) async-start(), calls=%async_computation.2 | async-start | bytes 4325376 | tf_op jit(solution)/shard_map/all_gather | solution.py:48
  7.9 147.3 %all-gather.11.cloned.1.call-start = ((), (), s32[]{:S(2)}) async-start(), calls=%async_computation.1 | async-start | bytes 1966080 | tf_op jit(solution)/shard_map/all_gather | solution.py:25
  8.7 195.0 %all-gather.15.cloned.1.call-start = ((), (), s32[]{:S(2)}) async-start(), calls=%async_computation.3 | async-start | bytes 1966080 | tf_op jit(solution)/shard_map/all_gather | solution.py:26
  9.4 242.6 %all-gather.17.cloned.1.call-start = ((), (), s32[]{:S(2)}) async-start(), calls=%async_computation.4 | async-start | bytes 1966080 | tf_op jit(solution)/shard_map/all_gather | solution.py:76
  10.0 291.0 %all-gather.19.cloned.1.call-start = ((), (), s32[]{:S(2)}) async-start(), calls=%async_computation.6 | async-start | bytes 1966080 | tf_op jit(solution)/shard_map/all_gather | solution.py:77
  115.1 327.2 %reduce-scatter.2.cloned.1.call-start = ((), (), s32[]{:S(2)}) async-start(), calls=%async_computation.5 | async-start | bytes 4325376 | tf_op jit(solution)/shard_map/reduce_scatter | solution.py:53
  156.9 50.3 %copy-start.2 = (bf16[1,768,1024]{1,2,0:T(8,128)(2,1)}, bf16[1,768,1024]{1,2,0:T(8,128)(2,1)S(1)}, u32[]{:S(2)}) copy-start(bf16[1,768,1024]{1,2,0:T(8,128)(2,1)S(1)} %copy.28) | copy-start | bytes 4718596
  206.3 2.3 copy-start.6
  207.3 4.2 copy-start.1
  207.3 2.6 copy-start.3
  211.5 3.4 copy-start.4
  211.5 3.5 copy-start.5
  256.7 44.3 %copy-start.7 = (bf16[24,8,8,128]{3,2,1,0:T(8,128)(2,1)S(1)}, bf16[24,8,8,128]{3,2,1,0:T(8,128)(2,1)}, u32[]{:S(2)}) copy-start(bf16[24,8,8,128]{3,2,1,0:T(8,128)(2,1)} %copy.67) | copy-start | bytes 1179652
Sparse Core Ops, SparseCore 0:
  11.1 99.4 all-gather.12
  112.7 42.4 all-gather.10
  157.3 46.2 all-gather.14
  205.6 46.3 all-gather.16
  254.5 46.4 all-gather.18
  305.4 136.9 reduce-scatter.1
where the time goes:
time: 532 us; the launch traced here: 531 us
  waiting for transfers between devices  351 us (66%)
  blocking collectives  117 us (22%)
  matrix products  28.8 us (5%)
  local copies, waits for them, and re-layouts  16.2 us (3%)
  between operations  15 us (3%)
    reduce_scatter x1, waiting for transfers between devices, shards(): lax.psum_scatter(lax.dot_general(attended_flat, grad_rows, (((0,), (0,)),...  130 us
    all_gather x1, waiting for transfers between devices, shards(): lax.all_gather(out_weight, 'fsdp', axis=0, tiled=True)  86.7 us
    psum x1, blocking collectives, shards(): lax.psum(weight_shard, ('seq', 'dp')) * (1.0 / math.sqrt(token_count))  81.5 us
    all_gather x1, waiting for transfers between devices, shards(): lax.all_gather(value, 'seq', axis=1, tiled=True)  46.7 us
    all_gather x1, waiting for transfers between devices, shards(): lax.all_gather(key, 'seq', axis=1, tiled=True)  39.8 us
    all_gather x1, waiting for transfers between devices, shards(): lax.all_gather(query, 'seq', axis=1, tiled=True)  22.9 us
    all_gather x1, waiting for transfers between devices, shards(): lax.all_gather(attn_grad[None], 'seq', axis=1, tiled=True)  22.4 us
    all_gather x1, blocking collectives, shards(): lax.all_gather(row_delta[None], 'seq', axis=2, tiled=True)  13.4 us
  transfers between devices with their start and end apart: 6, of which 6 were waited for; matrix products, arithmetic and copies ran while one was open for 9% of the time, Pallas kernels for 0%

commit v1 on v0

--- a/solution.py
+++ b/solution.py
@@ -59,9 +59,10 @@
         tiled=True,
     ).astype(jnp.float32)
     token_count = tokens_here * lax.axis_size("seq") * lax.axis_size("fsdp") * lax.axis_size("dp")
-    weight_grad = (lax.psum(weight_shard, ("seq", "dp")) * (1.0 / math.sqrt(token_count))).astype(
-        jnp.bfloat16
-    )
+    weight_grad = (
+        jnp.sum(lax.all_gather(weight_shard, axis_name=("seq", "dp")), 0)
+        * (1.0 / math.sqrt(token_count))
+    ).astype(jnp.bfloat16)
     grad_heads = attn_grad.reshape(tokens_here, HEADS, HD)
     row_delta = jnp.einsum("thd,thd->ht", grad_heads, attended, preferred_element_type=jnp.float32)
     prob_grad = jnp.einsum(

time: 532 us -> 551 us (1.036)
  the two profiles are of different devices: /device:TPU:16 before, /device:TPU:2 now
where the time goes in v1:
time: 551 us
  waiting for transfers between devices  445 us (81%)
  blocking collectives  35.6 us (6%)
  matrix products  30.1 us (5%)
  local copies, waits for them, and re-layouts  17.1 us (3%)
  between operations  15 us (3%)
  other arithmetic  7.08 us (1%)
    reduce_scatter x1, waiting for transfers between devices, shards(): lax.psum_scatter(lax.dot_general(attended_flat, grad_rows, (((0,), (0,)),...  133 us
    all_gather x1, waiting for transfers between devices, shards(): lax.all_gather(out_weight, 'fsdp', axis=0, tiled=True)  90.8 us
    all_gather x1, waiting for transfers between devices, shards(): lax.all_gather(weight_shard, axis_name=('seq', 'dp'))  83.5 us
    all_gather x1, waiting for transfers between devices, shards(): lax.all_gather(value, 'seq', axis=1, tiled=True)  46.7 us
    all_gather x1, waiting for transfers between devices, shards(): lax.all_gather(key, 'seq', axis=1, tiled=True)  37.8 us
    all_gather x1, waiting for transfers between devices, shards(): lax.all_gather(query, 'seq', axis=1, tiled=True)  27.5 us
    all_gather x1, waiting for transfers between devices, shards(): lax.all_gather(attn_grad[None], 'seq', axis=1, tiled=True)  22.6 us
    all_gather x1, blocking collectives, shards(): lax.all_gather(row_delta[None], 'seq', axis=2, tiled=True)  13.4 us
  transfers between devices with their start and end apart: 7, of which 7 were waited for; matrix products, arithmetic and copies ran while one was open for 7% of the time, Pallas kernels for 0%

profile of v1, /device:TPU:2, one launch (start us, length us, event | category | flops | bytes accessed | tf_op | source)
XLA Modules:
  0.0 550.5 jit_solution(11012804662886660687)
XLA Ops:
  7.2 0.7 all-gather.13.cloned.1.call-update
  8.0 0.7 all-gather.17.cloned.1.call-update
  8.7 0.7 all-gather.15.cloned.1.call-update
  9.4 1.3 dynamic-slice
  11.4 0.9 dynamic-update-slice
  12.2 9.1 %all-reduce = s32[8]{0:T(128)S(1)} all-reduce(s32[8]{0:T(128)S(1)} %dynamic-update-slice), channel_id=1, replica_groups=mesh['seq'=4,'fsdp'=32,'dp'=4] {'seq'}, use_global_device_ids=true, to_apply=%add | all-reduce | flops 8 | bytes 64
  21.4 0.1 add.63
  21.5 0.7 broadcast_multiply_fusion
  22.2 0.1 add.67
  22.3 1.1 copy.64
  23.4 0.2 broadcast_compare_fusion
  23.6 37.8 %all-gather.13.cloned.1.call-done = bf16[1,768,1024]{2,1,0:T(8,128)(2,1)} async-done(((bf16[1,192,1024]{2,1,0:T(8,128)(2,1)}), bf16[1,768,1024]{2,1,0:T(8,128)(2,1)}) %all-gather.13.cloned.1.call-update) | async-done | bytes 1572880 | tf_op jit(solution)/shard_map/all_gather | solution.py:25
  61.4 1.7 copy.28
  63.1 46.7 %all-gather.17.cloned.1.call-done = bf16[1,768,1024]{2,1,0:T(8,128)(2,1)} async-done(((bf16[1,192,1024]{2,1,0:T(8,128)(2,1)}), bf16[1,768,1024]{2,1,0:T(8,128)(2,1)}) %all-gather.17.cloned.1.call-update) | async-done | bytes 1572880 | tf_op jit(solution)/shard_map/all_gather | solution.py:26
  109.8 2.6 copy.31
  112.4 1.0 fusion.3
  113.5 2.1 copy-done.1
  115.6 1.2 exponential_reduce_fusion
  116.8 90.8 %all-gather.15.cloned.1.call-done = bf16[1024,2048]{1,0:T(8,128)(2,1)} async-done(((bf16[32,2048]{1,0:T(8,128)(2,1)}), bf16[1024,2048]{1,0:T(8,128)(2,1)}) %all-gather.15.cloned.1.call-update) | async-done | bytes 4194320 | tf_op jit(solution)/shard_map/all_gather | solution.py:48
  207.6 3.7 convolution_convert_fusion.1
  211.4 0.1 bitcast_convert_fusion
  211.5 3.9 multiply_reduce_fusion
  215.4 3.3 convolution_convert_fusion
  218.8 0.5 all-gather.19.cloned.1.call-update
  219.4 0.5 all-gather.21.cloned.1.call-update
  219.9 133.3 %reduce-scatter.2.cloned.1.call-done = bf16[32,2048]{1,0:T(8,128)(2,1)} async-done(((bf16[1024,2048]{1,0:T(8,128)(2,1)}), bf16[32,2048]{1,0:T(8,128)(2,1)}) %reduce-scatter.2.cloned.1.call-update) | async-done | bytes 131088 | tf_op jit(solution)/shard_map/reduce_scatter | solution.py:53
  353.2 1.6 all_gather.44
  355.0 0.8 copy.67
  355.8 13.1 %all-gather.4 = f32[4,192,8]{1,2,0:T(8,128)S(1)} all-gather(f32[1,192,8]{1,2,0:T(8,128)S(1)} %bitcast.117), channel_id=2, replica_groups=mesh['seq'=4,'fsdp'=32,'dp'=4] {'seq'}, dimensions={0}, use_global_device_ids=true | all-gather | bytes 30720 | tf_op jit(solution)/shard_map/all_gather | solution.py:81
  369.0 0.1 reshape.142
  369.0 27.5 %all-gather.19.cloned.1.call-done = bf16[1,768,1024]{2,1,0:T(8,128)(2,1)} async-done(((bf16[1,192,1024]{2,1,0:T(8,128)(2,1)}), bf16[1,768,1024]{2,1,0:T(8,128)(2,1)}) %all-gather.19.cloned.1.call-update) | async-done | bytes 1572880 | tf_op jit(solution)/shard_map/all_gather | solution.py:77
  396.5 1.7 copy.37
  398.2 2.9 fusion.72
  401.1 6.3 %fusion.56 = bf16[192,8,128]{2,0,1:T(8,128)(2,1)} fusion(bf16[768,8,128]{0,2,1:T(8,128)(2,1)} %bitcast.106, f32[8,192,768]{2,1,0:T(8,128)} %copy-done.1, f32[8,192]{1,0:T(8,128)S(1)} %get-tuple-element.8, f32[8,192]{1,0:T(8,128)S(1)} %log_add_fusion, pred[192,768]{1,0:T(8,128)(4,1)S(1)} %get-tuple-element.5, bf16[768,8,128]{0,2,1:T(8,128)(2,1)} %bitcast.108, ...), kind=kOutput, calls=%fused_computation.39 | convolution fusion | flops 611450880 | bytes 8810496 | tf_op jit(solution)/shard_map/htk,khd->thd/dot_general | solution.py:73
  407.4 1.3 copy.36
  408.7 0.9 broadcast_in_dim_reshape.6
  409.6 13.4 %all-gather.5 = f32[4,192,8]{1,2,0:T(8,128)S(1)} all-gather(f32[1,192,8]{1,2,0:T(8,128)S(1)} %bitcast.121), channel_id=4, replica_groups=mesh['seq'=4,'fsdp'=32,'dp'=4] {'seq'}, dimensions={0}, use_global_device_ids=true | all-gather | bytes 30720 | tf_op jit(solution)/shard_map/all_gather | solution.py:82
  423.0 0.1 reshape.144
  423.1 22.6 %all-gather.21.cloned.1.call-done = bf16[768,1024]{1,0:T(8,128)(2,1)} async-done(((bf16[192,1024]{1,0:T(8,128)(2,1)}), bf16[768,1024]{1,0:T(8,128)(2,1)}) %all-gather.21.cloned.1.call-update) | async-done | bytes 1572880 | tf_op jit(solution)/shard_map/all_gather | solution.py:78
  445.7 4.8 fusion.51
  450.5 0.3 copy.45
  450.8 0.9 broadcast_in_dim_reshape.14
  451.7 4.2 fusion.57
  455.9 0.3 copy.47
  456.2 0.9 broadcast_in_dim_reshape.15
  457.1 83.5 %all-gather.23.cloned.1.call-done = f32[512,2048]{1,0:T(8,128)} async-done(((f32[32,2048]{1,0:T(8,128)}), f32[512,2048]{1,0:T(8,128)}) %all-gather.23.cloned.1.call-update) | async-done | bytes 4194320 | tf_op jit(solution)/shard_map/all_gather | solution.py:63
  540.6 2.4 reduce_sum.19
  543.0 0.7 multiply_convert_fusion.8
  (35 shorter events, 0.7 us)
Async XLA Ops:
  7.2 200.5 %copy-start = (bf16[1,192,2048]{2,1,0:T(8,128)(2,1)S(1)}, bf16[1,192,2048]{2,1,0:T(8,128)(2,1)}, u32[]{:S(2)}) copy-start(bf16[1,192,2048]{2,1,0:T(8,128)(2,1)} %param.10) | copy-start | bytes 2359300
  7.2 54.2 %all-gather.13.cloned.1.call-start = ((), (), s32[]{:S(2)}) async-start(), calls=%async_computation.1 | async-start | bytes 1966080 | tf_op jit(solution)/shard_map/all_gather | solution.py:25
  7.9 101.9 %all-gather.17.cloned.1.call-start = ((), (), s32[]{:S(2)}) async-start(), calls=%async_computation.3 | async-start | bytes 1966080 | tf_op jit(solution)/shard_map/all_gather | solution.py:26
  8.7 199.0 %all-gather.15.cloned.1.call-start = ((), (), s32[]{:S(2)}) async-start(), calls=%async_computation.2 | async-start | bytes 4325376 | tf_op jit(solution)/shard_map/all_gather | solution.py:48
  9.4 343.9 %reduce-scatter.2.cloned.1.call-start = ((), (), s32[]{:S(2)}) async-start(), calls=%async_computation.5 | async-start | bytes 4325376 | tf_op jit(solution)/shard_map/reduce_scatter | solution.py:53
  63.1 50.3 %copy-start.2 = (bf16[1,768,1024]{1,2,0:T(8,128)(2,1)}, bf16[1,768,1024]{1,2,0:T(8,128)(2,1)S(1)}, u32[]{:S(2)}) copy-start(bf16[1,768,1024]{1,2,0:T(8,128)(2,1)S(1)} %copy.28) | copy-start | bytes 4718596
  113.5 2.1 copy-start.1
  116.8 94.7 %copy-start.3 = (bf16[1,768,1024]{1,2,0:T(8,128)(2,1)S(1)}, bf16[1,768,1024]{1,2,0:T(8,128)(2,1)}, u32[]{:S(2)}) copy-start(bf16[1,768,1024]{1,2,0:T(8,128)(2,1)} %copy.31) | copy-start | bytes 4718596
  211.4 4.1 copy-start.6
  218.7 136.2 %copy-start.4 = (bf16[1,192,1024]{2,1,0:T(8,128)(2,1)S(1)}, bf16[1,192,1024]{2,1,0:T(8,128)(2,1)}, u32[]{:S(2)}) copy-start(bf16[1,192,1024]{2,1,0:T(8,128)(2,1)} %param.7) | copy-start | bytes 1179652
  218.7 136.3 %copy-start.5 = (bf16[1,192,1024]{2,1,0:T(8,128)(2,1)S(1)}, bf16[1,192,1024]{2,1,0:T(8,128)(2,1)}, u32[]{:S(2)}) copy-start(bf16[1,192,1024]{2,1,0:T(8,128)(2,1)} %param.8) | copy-start | bytes 1179652
  218.7 177.8 %all-gather.19.cloned.1.call-start = ((), (), s32[]{:S(2)}) async-start(), calls=%async_computation.4 | async-start | bytes 1966080 | tf_op jit(solution)/shard_map/all_gather | solution.py:77
  219.3 226.3 %all-gather.21.cloned.1.call-start = ((), (), s32[]{:S(2)}) async-start(), calls=%async_computation.6 | async-start | bytes 1966080 | tf_op jit(solution)/shard_map/all_gather | solution.py:78
  219.9 320.7 %all-gather.23.cloned.1.call-start = ((), (), s32[]{:S(2)}) async-start(), calls=%async_computation.7 | async-start | bytes 4456448 | tf_op jit(solution)/shard_map/all_gather | solution.py:63
  369.0 32.1 %copy-start.7 = (bf16[192,1024]{1,0:T(8,128)(2,1)S(1)}, bf16[192,1024]{1,0:T(8,128)(2,1)}, u32[]{:S(2)}) copy-start(bf16[192,1024]{1,0:T(8,128)(2,1)} %copy-done.6) | copy-start | bytes 1179652
  401.1 44.5 %copy-start.8 = (bf16[24,8,8,128]{3,2,1,0:T(8,128)(2,1)S(1)}, bf16[24,8,8,128]{3,2,1,0:T(8,128)(2,1)}, u32[]{:S(2)}) copy-start(bf16[24,8,8,128]{3,2,1,0:T(8,128)(2,1)} %copy.67) | copy-start | bytes 1179652
Sparse Core Ops, SparseCore 0:
  10.1 51.2 all-gather.12
  63.5 46.2 all-gather.16
  113.0 94.6 all-gather.14
  218.9 134.3 reduce-scatter.1
  355.4 41.0 all-gather.18
  399.3 46.3 all-gather.20
  448.0 92.5 all-gather.22
